TPU v7x, 128 devices: a whole 4x4x4 slice. The times are simulated.
128 devices in a mesh: ctx: 16 (over x, z_hi, core), tp: 8 (over y, z_lo).
Axes of the slice: x: 4, y: 4, z: 4 (z_hi: 2, z_lo: 2; z = z_hi * 2 + z_lo), core: 2. Of those that a mesh axis runs over, the one named last changes fastest.
Arguments:
- query_proj: bfloat16 [6144, 4096], P('ctx', 'tp'), may hold values from -6 to 6
- key_proj: bfloat16 [6144, 4096], P('ctx', 'tp'), may hold values from -6 to 6
- value_proj: bfloat16 [6144, 4096], P('ctx', 'tp'), may hold values from -6 to 6
- saved_conv: bfloat16 [6144, 4096], P('ctx', 'tp'), may hold values from -6 to 6
- grad_out: bfloat16 [6144, 4096], P(('ctx', 'tp')), may hold values from -6 to 6
- filters: bfloat16 [256, 6144], P('tp'), may hold values from -0.109375 to 0.109375
- featurizer: float32 [3, 3, 4096], P(None, None, 'tp'), may hold values from -2 to 2
Outputs:
- grad_query: bfloat16 [6144, 4096], P('ctx', 'tp')
- grad_key: bfloat16 [6144, 4096], P('ctx', 'tp')
- grad_value: bfloat16 [6144, 4096], P('ctx', 'tp')
All inputs are finite; a program needn't handle non-finite values.
Results may differ from a plain program's by a relative error of at most 0.012.
Values may be sent and summed in bfloat16 or wider, within the bound.
A program may use at most 256 MiB of HBM per device.

v0:
```python
import jax
import jax.numpy as jnp
from jax import lax
from jax.sharding import PartitionSpec as P

GSIZE = 16
TAPS = 3


def shifted(array, axis, by):
    length = lax.axis_size(axis)
    pairs = [(i, i + by) for i in range(length) if 0 <= i + by < length]
    return lax.ppermute(array, axis, pairs)


def featurize(current, previous, kernel):
    amount = current.shape[0]
    joined = jnp.concatenate([previous, current], axis=0).astype(jnp.float32)
    total = kernel[0] * joined[TAPS - 1 : TAPS - 1 + amount]
    for offset in range(1, TAPS):
        total = total + kernel[offset] * joined[TAPS - 1 - offset : TAPS - 1 - offset + amount]
    return total


def spread(current, following, kernel):
    amount = current.shape[0]
    joined = jnp.concatenate([current, following], axis=0)
    total = kernel[0] * joined[0:amount]
    for offset in range(1, TAPS):
        total = total + kernel[offset] * joined[offset : offset + amount]
    return total


def toeplitz_tiles(window, tile_rows, width_k):
    groups = window.shape[0]
    padded = jnp.concatenate([window, jnp.zeros((groups, 1), window.dtype)], axis=1)
    tiled = jnp.tile(padded, (1, tile_rows))
    folded = tiled[:, : tile_rows * (width_k + tile_rows - 1)].reshape(
        groups, tile_rows, width_k + tile_rows - 1
    )
    return folded[:, :, tile_rows - 1 : tile_rows - 1 + width_k]


def cross_terms(source, src_start, dst_start, dst_rows, filt_pad, front_pad, tile_rows):
    groups = filt_pad.shape[0]
    src_rows = source.shape[0]
    src_tiles = -(-src_rows // tile_rows)
    dst_tiles = dst_rows // tile_rows
    width_k = (dst_tiles + src_tiles - 1) * tile_rows
    lag_first = src_start - dst_start - (dst_tiles - 1) * tile_rows - (tile_rows - 1)
    window = lax.dynamic_slice_in_dim(filt_pad, lag_first + front_pad, width_k + tile_rows - 1, 1)
    tiles = toeplitz_tiles(window, tile_rows, width_k)
    pieces = source.reshape(src_tiles, tile_rows, groups, GSIZE)
    result = jnp.zeros((dst_tiles, tile_rows, groups, GSIZE), jnp.float32)
    for diagonal in range(dst_tiles + src_tiles - 1):
        offset = diagonal - (dst_tiles - 1)
        lowest = max(0, -offset)
        highest = min(dst_tiles, src_tiles - offset)
        matrix = tiles[:, :, diagonal * tile_rows : (diagonal + 1) * tile_rows]
        product = jnp.einsum(
            "gij,ajgc->aigc",
            matrix,
            pieces[lowest + offset : highest + offset],
            preferred_element_type=jnp.float32,
        )
        result = result.at[lowest:highest].add(product)
    return result.reshape(dst_rows, groups * GSIZE)


def body(query_proj, key_proj, value_proj, saved_conv, grad_out, filters, featurizer):
    block_rows, channels = query_proj.shape
    tokens = filters.shape[1]
    tile_rows = min(128, block_rows)
    own_start = lax.axis_index("ctx") * block_rows
    front_pad = 2 * tokens
    filt_pad = jnp.pad(filters, ((0, 0), (front_pad, tokens + 2 * tile_rows)))
    upstream = lax.all_to_all(grad_out, "tp", split_axis=1, concat_axis=0, tiled=True)
    previous = shifted(
        (
            query_proj[block_rows - (TAPS - 1) :],
            key_proj[block_rows - (TAPS - 1) :],
            value_proj[block_rows - (TAPS - 1) :],
        ),
        "ctx",
        1,
    )
    query_feat = featurize(query_proj, previous[0], featurizer[0])
    key_feat = featurize(key_proj, previous[1], featurizer[1])
    value_feat = featurize(value_proj, previous[2], featurizer[2])
    upstream_f = upstream.astype(jnp.float32)
    grad_qfeat = upstream_f * saved_conv.astype(jnp.float32)
    grad_conv = (upstream_f * query_feat).astype(jnp.bfloat16)
    empty = jnp.zeros((block_rows, channels), jnp.float32)
    piece = lax.all_gather(grad_conv, "ctx", axis=0, tiled=True)
    piece_start = jnp.int32(0)
    grad_mix = lax.cond(
        piece_start + piece.shape[0] > own_start,
        lambda: cross_terms(
            piece, piece_start, own_start, block_rows, filt_pad, front_pad, tile_rows
        ),
        lambda: empty,
    )
    grad_kfeat = grad_mix * value_feat
    grad_vfeat = grad_mix * key_feat
    following = shifted(
        (grad_qfeat[: TAPS - 1], grad_kfeat[: TAPS - 1], grad_vfeat[: TAPS - 1]), "ctx", -1
    )
    grad_query = spread(grad_qfeat, following[0], featurizer[0]).astype(jnp.bfloat16)
    grad_key = spread(grad_kfeat, following[1], featurizer[1]).astype(jnp.bfloat16)
    grad_value = spread(grad_vfeat, following[2], featurizer[2]).astype(jnp.bfloat16)
    return (grad_query, grad_key, grad_value)


def solution(mesh):
    return jax.shard_map(
        body,
        mesh=mesh,
        in_specs=(
            P("ctx", "tp"),
            P("ctx", "tp"),
            P("ctx", "tp"),
            P("ctx", "tp"),
            P(("ctx", "tp"), None),
            P("tp", None),
            P(None, None, "tp"),
        ),
        out_specs=(P("ctx", "tp"), P("ctx", "tp"), P("ctx", "tp")),
        check_vma=False,
    )
```

profile of v0, /device:TPU:1, one launch (start us, length us, event | category | flops | bytes accessed | tf_op | source)
XLA Modules:
  0.0 704.6 jit_solution(5903635782921676362)
XLA Ops:
  7.9 6.9 collective-permute-start.1
  16.5 4.6 all-to-all-start
  23.8 4.0 all-to-all-done
  30.7 5.2 collective-permute-start.2
  45.7 48.6 %all-gather.2.cloned.1.call-done = bf16[6144,512]{1,0:T(8,128)(2,1)} async-done(((bf16[384,512]{1,0:T(8,128)(2,1)}), bf16[6144,512]{1,0:T(8,128)(2,1)}) %all-gather.2.cloned.1.call-update) | async-done | bytes 6291472 | tf_op jit(solution)/shard_map/all_gather | solution.py:94
  94.4 589.0 %conditional.1 = (f32[384,512]{1,0:T(8,128)}) conditional(s32[]{:T(128)} %convert_element_type.43, () %tuple.355, (bf16[32,6144]{1,0:T(8,128)(2,1)}, s32[]{:T(128)}, bf16[6144,512]{1,0:T(8,128)(2,1)}) %tuple.356), branch_computations={%region_0.1_spmd, %region_1.2_spmd} | conditional | flops 2425290752 | bytes 657653696 | solution.py:96
  95.8 17.2 %tile.1 = bf16[32,128,6528]{2,1,0:T(8,128)(2,1)} broadcast(bf16[32,6528]{1,0:T(8,128)(2,1)S(1)} %concatenate.114), dimensions={0,2} | broadcast | bytes 53895168 | tf_op jit(solution)/shard_map/cond/branch_1_fun/tile | solution.py:37
  113.0 49.0 %copy.164 = bf16[4,8,128,6528]{3,1,2,0:T(8,128)(2,1)} copy(bf16[4,8,128,6528]{3,2,1,0:T(8,128)(2,1)} %bitcast.572) | data formatting | bytes 106954752 | tf_op jit(solution)/shard_map/cond
  162.0 35.7 %slice.1975 = bf16[32,835456]{1,0:T(8,128)(2,1)} slice(bf16[32,835584]{1,0:T(8,128)(2,1)} %bitcast.573), slice={[0:32], [0:835456]} | slice | bytes 106938368 | tf_op jit(solution)/shard_map/cond/branch_1_fun/slice | solution.py:38
  197.7 208.9 %reshape.2132 = bf16[32,128,6527]{2,1,0:T(8,128)(2,1)} reshape(bf16[32,835456]{1,0:T(8,128)(2,1)} %slice.1975) | data formatting | bytes 106938368 | tf_op jit(solution)/shard_map/cond/branch_1_fun/reshape | solution.py:38
  406.5 8.9 %copy.159 = bf16[6144,512]{0,1:T(8,128)(2,1)} copy(bf16[6144,512]{1,0:T(8,128)(2,1)} %get-tuple-element.998) | data formatting | bytes 12582912 | tf_op jit(solution)/shard_map
  416.6 2.3 fusion.97
  423.1 6.3 fusion.131
  430.9 3.4 fusion.95
  434.3 6.4 fusion.132
  442.1 3.4 fusion.49
  447.0 3.4 fusion.47
  451.9 3.4 fusion.45
  456.8 3.4 fusion.43
  461.6 3.4 fusion.41
  466.5 3.4 fusion.39
  471.8 3.4 fusion.37
  476.7 3.4 fusion.35
  481.5 3.4 fusion.33
  486.4 3.4 fusion.31
  491.3 3.4 fusion.93
  496.2 3.4 fusion.29
  501.0 3.4 fusion.27
  505.9 3.4 fusion.25
  510.8 3.4 fusion.23
  515.6 3.4 fusion.21
  520.7 3.4 fusion.19
  525.5 3.4 fusion.17
  530.4 3.4 fusion.15
  535.3 3.4 fusion.13
  540.2 3.4 fusion.11
  545.1 3.4 fusion.9
  549.9 3.4 fusion.7
  554.8 3.4 fusion.5
  559.7 3.5 fusion.75
  564.6 3.4 fusion.73
  569.7 3.4 fusion.71
  574.6 3.4 fusion.69
  579.4 3.4 fusion.67
  584.3 3.4 fusion.65
  589.2 3.4 fusion.63
  594.0 3.4 fusion.61
  598.9 3.4 fusion.59
  603.8 3.4 fusion.57
  608.7 3.4 fusion.55
  613.5 3.4 fusion.53
  618.8 3.4 fusion.51
  622.2 3.7 fusion.133
  627.4 3.4 fusion.91
  632.2 3.4 fusion.89
  637.1 3.4 fusion.87
  642.0 3.4 fusion.85
  646.9 3.4 fusion.83
  651.7 3.4 fusion.81
  656.6 3.4 fusion.79
  661.5 2.5 fusion.77
  664.0 12.7 %bitcast_add_fusion = f32[3,128,32,16]{1,3,2,0:T(8,128)S(1)} fusion(f32[3,128,32,16]{1,3,2,0:T(8,128)S(1)} %fusion.100, f32[32,128,3,16]{1,3,2,0:T(8,128)} %bitcast.600, f32[32,128,3,16]{1,3,2,0:T(8,128)} %bitcast.599, f32[32,128,3,16]{1,3,2,0:T(8,128)} %bitcast.598, f32[32,128,3,16]{1,3,2,0:T(8,128)} %bitcast.597, f32[32,128,3,16]{1,3,2,0:T(8,128)} %bitcast.596, ...), kind=kLoop, calls=%fused_computation.104 | loop fusion | flops 9043968 | bytes 37748736 | tf_op jit(solution)/shard_map/cond/branch_1_fun/add | solution.py:66
  687.4 2.8 fusion.115
  693.1 3.5 collective-permute-done.3
  (159 shorter events, 106.7 us)
Async XLA Ops:
  7.9 14.8 %collective-permute-start.1 = (bf16[2,512]{1,0:T(2,128)(2,1)S(1)}, bf16[2,512]{1,0:T(2,128)(2,1)S(1)}, u32[]{:S(2)}, u32[]{:S(2)}) collective-permute-start(bf16[2,512]{1,0:T(2,128)(2,1)S(1)} %slice.1952), channel_id=1, source_target_pairs={{0,8},{8,16},{16,24},{24,32},{32,40},{40,48},{48,56},{56,64},{64,7... | collective-permute-start | bytes 6152 | tf_op jit(solution)/shard_map/ppermute | solution.py:13
  16.5 11.3 %all-to-all-start = ((bf16[48,8,512]{2,0,1:T(8,128)(2,1)}), bf16[48,8,512]{2,0,1:T(8,128)(2,1)S(1)}, u32[]{:S(2)}, u32[]{:S(2)}) async-start(bf16[48,8,512]{2,0,1:T(8,128)(2,1)} %bitcast.571), calls=%async_computation | async-start | bytes 786432 | tf_op jit(solution)/shard_map/all_to_all | solution.py:77
  21.2 73.2 %all-gather.2.cloned.1.call-start = ((), (), s32[]{:S(2)}) async-start(), calls=%async_computation.1 | async-start | bytes 6684672 | tf_op jit(solution)/shard_map/all_gather | solution.py:94
  22.7 71.7 %copy-start.3 = (f32[1,1,512]{2,1,0:T(1,128)}, f32[1,1,512]{2,1,0:T(1,128)S(1)}, u32[]{:S(2)}) copy-start(f32[1,1,512]{2,1,0:T(1,128)S(1)} %get-tuple-element.1060) | copy-start | bytes 6148
  22.7 71.7 %copy-start.4 = (f32[1,1,512]{2,1,0:T(1,128)}, f32[1,1,512]{2,1,0:T(1,128)S(1)}, u32[]{:S(2)}) copy-start(f32[1,1,512]{2,1,0:T(1,128)S(1)} %get-tuple-element.1061) | copy-start | bytes 6148
  22.7 71.7 %copy-start.5 = (f32[1,1,512]{2,1,0:T(1,128)}, f32[1,1,512]{2,1,0:T(1,128)S(1)}, u32[]{:S(2)}) copy-start(f32[1,1,512]{2,1,0:T(1,128)S(1)} %get-tuple-element.1062) | copy-start | bytes 6148
  30.0 64.4 %copy-start.2 = (f32[384,512]{1,0:T(8,128)}, f32[384,512]{1,0:T(8,128)S(1)}, u32[]{:S(2)}) copy-start(f32[384,512]{1,0:T(8,128)S(1)} %get-tuple-element.1055) | copy-start | bytes 2359300
  30.7 8.0 %collective-permute-start.2 = (bf16[2,512]{1,0:T(2,128)(2,1)S(1)}, bf16[2,512]{1,0:T(2,128)(2,1)S(1)}, u32[]{:S(2)}, u32[]{:S(2)}) collective-permute-start(bf16[2,512]{1,0:T(2,128)(2,1)S(1)} %slice.1957), channel_id=1, source_target_pairs={{0,8},{8,16},{16,24},{24,32},{32,40},{40,48},{48,56},{56,64},{64,7... | collective-permute-start | bytes 6152 | tf_op jit(solution)/shard_map/ppermute | solution.py:13
  36.7 4.2 collective-permute-start.4
  43.5 643.9 %collective-permute-start = (f32[2,512]{1,0:T(2,128)}, f32[2,512]{1,0:T(2,128)}, u32[]{:S(2)}, u32[]{:S(2)}) collective-permute-start(f32[2,512]{1,0:T(2,128)} %slice.2078), channel_id=1, source_target_pairs={{8,0},{16,8},{24,16},{32,24},{40,32},{48,40},{56,48},{64,56},{72,6... | collective-permute-start | bytes 12296 | tf_op jit(solution)/shard_map/ppermute | solution.py:13
  94.4 589.1 %copy-start = (f32[386,512]{1,0:T(8,128)S(1)}, f32[386,512]{1,0:T(8,128)}, u32[]{:S(2)}) copy-start(f32[386,512]{1,0:T(8,128)} %maximum_convert_fusion.1) | copy-start | bytes 2371588
  94.4 589.1 %copy-start.1 = (f32[386,512]{1,0:T(8,128)S(1)}, f32[386,512]{1,0:T(8,128)}, u32[]{:S(2)}) copy-start(f32[386,512]{1,0:T(8,128)} %maximum_convert_fusion.2) | copy-start | bytes 2371588
  94.4 589.1 %copy-start.6 = (f32[1,1,512]{2,1,0:T(1,128)S(1)}, f32[1,1,512]{2,1,0:T(1,128)}, u32[]{:S(2)}) copy-start(f32[1,1,512]{2,1,0:T(1,128)} %get-tuple-element.1056) | copy-start | bytes 6148
  94.4 589.1 %copy-start.7 = (f32[1,1,512]{2,1,0:T(1,128)S(1)}, f32[1,1,512]{2,1,0:T(1,128)}, u32[]{:S(2)}) copy-start(f32[1,1,512]{2,1,0:T(1,128)} %get-tuple-element.1063) | copy-start | bytes 6148
  94.4 589.1 %copy-start.8 = (f32[1,1,512]{2,1,0:T(1,128)S(1)}, f32[1,1,512]{2,1,0:T(1,128)}, u32[]{:S(2)}) copy-start(f32[1,1,512]{2,1,0:T(1,128)} %get-tuple-element.1064) | copy-start | bytes 6148
  94.4 589.1 %copy-start.9 = (f32[1,1,512]{2,1,0:T(1,128)S(1)}, f32[1,1,512]{2,1,0:T(1,128)}, u32[]{:S(2)}) copy-start(f32[1,1,512]{2,1,0:T(1,128)} %get-tuple-element.1057) | copy-start | bytes 6148
  94.4 589.1 %copy-start.10 = (f32[1,1,512]{2,1,0:T(1,128)S(1)}, f32[1,1,512]{2,1,0:T(1,128)}, u32[]{:S(2)}) copy-start(f32[1,1,512]{2,1,0:T(1,128)} %get-tuple-element.1058) | copy-start | bytes 6148
  94.4 589.1 %copy-start.11 = (f32[1,1,512]{2,1,0:T(1,128)S(1)}, f32[1,1,512]{2,1,0:T(1,128)}, u32[]{:S(2)}) copy-start(f32[1,1,512]{2,1,0:T(1,128)} %get-tuple-element.1059) | copy-start | bytes 6148
  685.2 6.9 collective-permute-start.5
  690.2 6.4 collective-permute-start.3
Sparse Core Ops, SparseCore 0:
  30.1 64.1 all-gather.1
where the time goes:
time: 712 us; the launch traced here: 705 us
  local copies, waits for them, and re-layouts  416 us (58%)
  matrix products  165 us (23%)
  waiting for transfers between devices  56.2 us (8%)
  other arithmetic  26.8 us (4%)
  starting transfers between devices  25.2 us (4%)
  between operations  14.4 us (2%)
    reshape x1, local copies, waits for them, and re-layouts, toeplitz_tiles(): tiled[:, :tile_rows * (width_k + tile_rows - 1)]  209 us
    cond x48, matrix products  161 us
    slice x101, local copies, waits for them, and re-layouts, cross_terms(): pieces[lowest + offset:highest + offset]  87 us
    cond x2, local copies, waits for them, and re-layouts  49.1 us
    all_gather x1, waiting for transfers between devices, body(): piece = lax.all_gather(grad_conv, 'ctx', axis=0, tiled=True)  48.6 us
    slice x1, local copies, waits for them, and re-layouts, toeplitz_tiles(): tiled[:, :tile_rows * (width_k + tile_rows - 1)]  35.7 us
    ppermute x6, starting transfers between devices, shifted(): return lax.ppermute(array, axis, pairs)  20.5 us
    another operation x1, local copies, waits for them, and re-layouts, toeplitz_tiles(): tiled = jnp.tile(padded, (1, tile_rows))  17.2 us
  transfers between devices with their start and end apart: 8, of which 3 were waited for; matrix products, arithmetic and copies ran while one was open for 86% of the time, Pallas kernels for 0%

commit v1 on v0

--- a/solution.py
+++ b/solution.py
@@ -1,3 +1,4 @@
+import functools
 import jax
 import jax.numpy as jnp
 from jax import lax
@@ -5,6 +6,16 @@
 
 GSIZE = 16
 TAPS = 3
+
+
+def shape_digits_by_axis(buf, k_dim):
+    latest = lax.axis_size("ctx")
+    a_now = jnp.stack([buf] * latest)
+    carry = lax.all_to_all(a_now, axis_name="ctx", split_axis=0, concat_axis=0)
+    return jnp.concatenate(carry, axis=k_dim)
+
+
+_remake_marks = functools.partial(shape_digits_by_axis, k_dim=0)
 
 
 def shifted(array, axis, by):
@@ -91,7 +102,7 @@
     grad_qfeat = upstream_f * saved_conv.astype(jnp.float32)
     grad_conv = (upstream_f * query_feat).astype(jnp.bfloat16)
     empty = jnp.zeros((block_rows, channels), jnp.float32)
-    piece = lax.all_gather(grad_conv, "ctx", axis=0, tiled=True)
+    piece = _remake_marks(grad_conv)
     piece_start = jnp.int32(0)
     grad_mix = lax.cond(
         piece_start + piece.shape[0] > own_start,

time: 712 us -> 782 us (1.098)
  local copies, waits for them, and re-layouts: 416 us -> 458 us
  waiting for transfers between devices: 56.2 us -> 87.7 us
  between operations: 14.4 us -> 1.07 us
    all_to_all x0 -> x1, waiting for transfers between devices: none -> 62.8 us  [shape_digits_by_axis(): carry = lax.all_to_all(a_now, axis_name='ctx', split_axis=0, concat_axis=0)]
    all_gather x1 -> x0, waiting for transfers between devices: 48.6 us -> none  [body(): piece = lax.all_gather(grad_conv, 'ctx', axis=0, tiled=True)]
    cond x2 -> x34, local copies, waits for them, and re-layouts: 49.1 us -> 78 us
    ppermute x6, waiting for transfers between devices: 3.51 us -> 20.9 us  [shifted(): return lax.ppermute(array, axis, pairs)]
    another operation x1 -> x3, local copies, waits for them, and re-layouts: 8.87 us -> 23 us  [the longest x1 10.5 us: cross_terms(): pieces = source.reshape(src_tiles, tile_rows, groups, GSIZE)]
    slice x101 -> x37, local copies, waits for them, and re-layouts: 87 us -> 85.9 us  [cross_terms(): pieces[lowest + offset:highest + offset]]
  transfers between devices with their start and end apart: 8 -> 8, of which waited for: 3 -> 5; matrix products, arithmetic and copies ran while one was open for 86% -> 83% of each run, Pallas kernels for 0% -> 0%
where the time goes in v1:
time: 782 us; the launch traced here: 770 us
  local copies, waits for them, and re-layouts  458 us (59%)
  matrix products  165 us (21%)
  waiting for transfers between devices  87.7 us (11%)
  starting transfers between devices  32.8 us (4%)
  other arithmetic  24.9 us (3%)
    reshape x1, local copies, waits for them, and re-layouts, toeplitz_tiles(): tiled[:, :tile_rows * (width_k + tile_rows - 1)]  209 us
    cond x48, matrix products  161 us
    slice x37, local copies, waits for them, and re-layouts, cross_terms(): pieces[lowest + offset:highest + offset]  85.9 us
    cond x34, local copies, waits for them, and re-layouts  78 us
    all_to_all x1, waiting for transfers between devices, shape_digits_by_axis(): carry = lax.all_to_all(a_now, axis_name='ctx', split_axis=0, concat_axis=0)  62.8 us
    slice x1, local copies, waits for them, and re-layouts, toeplitz_tiles(): tiled[:, :tile_rows * (width_k + tile_rows - 1)]  35.7 us
    ppermute x6, waiting for transfers between devices, shifted(): return lax.ppermute(array, axis, pairs)  20.9 us
    ppermute x6, starting transfers between devices, shifted(): return lax.ppermute(array, axis, pairs)  20.4 us
  transfers between devices with their start and end apart: 8, of which 5 were waited for; matrix products, arithmetic and copies ran while one was open for 83% of the time, Pallas kernels for 0%

profile of v1, /device:TPU:1, one launch (start us, length us, event | category | flops | bytes accessed | tf_op | source)
XLA Modules:
  0.0 770.4 jit_solution(5871434824340911095)
XLA Ops:
  1.3 6.9 collective-permute-start.1
  10.0 4.6 all-to-all-start
  17.3 4.1 all-to-all-done
  22.9 3.4 stack.2
  26.4 7.8 %all-to-all-start.1 = ((bf16[16,384,512]{1,2,0:T(8,128)(2,1)}), bf16[16,384,512]{1,2,0:T(8,128)(2,1)}, u32[]{:S(2)}, u32[]{:S(2)}) async-start(bf16[16,384,512]{1,2,0:T(8,128)(2,1)} %stack.2), calls=%async_computation.1 | async-start | bytes 12582912 | tf_op jit(solution)/shard_map/all_to_all | solution.py:14
  34.8 5.0 collective-permute-start.4
  42.6 17.4 %collective-permute-done.4 = bf16[2,512]{1,0:T(2,128)(2,1)S(1)} collective-permute-done((bf16[2,512]{1,0:T(2,128)(2,1)S(1)}, bf16[2,512]{1,0:T(2,128)(2,1)S(1)}, u32[]{:S(2)}, u32[]{:S(2)}) %collective-permute-start.4) | collective-permute-done | bytes 2080 | tf_op jit(solution)/shard_map/ppermute | solution.py:24
  66.6 62.8 %all-to-all-done.1 = bf16[16,384,512]{1,2,0:T(8,128)(2,1)} async-done(((bf16[16,384,512]{1,2,0:T(8,128)(2,1)}), bf16[16,384,512]{1,2,0:T(8,128)(2,1)}, u32[]{:S(2)}, u32[]{:S(2)}) %all-to-all-start.1) | async-done | bytes 6291488 | tf_op jit(solution)/shard_map/all_to_all | solution.py:14
  129.4 627.2 %conditional.1 = (f32[384,512]{1,0:T(8,128)}) conditional(s32[]{:T(128)} %convert_element_type.43, () %tuple.355, (bf16[32,6144]{1,0:T(8,128)(2,1)}, s32[]{:T(128)}, bf16[16,384,512]{1,2,0:T(8,128)(2,1)}) %tuple.356), branch_computations={%region_0.1_spmd, %region_1.2_spmd} | conditional | flops 2425290752 | bytes 645726144 | solution.py:107
  130.8 17.2 %tile.1 = bf16[32,128,6528]{2,1,0:T(8,128)(2,1)} broadcast(bf16[32,6528]{1,0:T(8,128)(2,1)S(1)} %concatenate.114), dimensions={0,2} | broadcast | bytes 53895168 | tf_op jit(solution)/shard_map/cond/branch_1_fun/tile | solution.py:48
  148.0 49.0 %copy.232 = bf16[4,8,128,6528]{3,1,2,0:T(8,128)(2,1)} copy(bf16[4,8,128,6528]{3,2,1,0:T(8,128)(2,1)} %bitcast.512) | data formatting | bytes 106954752 | tf_op jit(solution)/shard_map/cond
  197.0 35.7 %slice.1877 = bf16[32,835456]{1,0:T(8,128)(2,1)} slice(bf16[32,835584]{1,0:T(8,128)(2,1)} %bitcast.513), slice={[0:32], [0:835456]} | slice | bytes 106938368 | tf_op jit(solution)/shard_map/cond/branch_1_fun/slice | solution.py:49
  232.7 209.0 %reshape.2065 = bf16[32,128,6527]{2,1,0:T(8,128)(2,1)} reshape(bf16[32,835456]{1,0:T(8,128)(2,1)} %slice.1877) | data formatting | bytes 106938368 | tf_op jit(solution)/shard_map/cond/branch_1_fun/reshape | solution.py:49
  441.8 9.1 %copy.92 = bf16[16,384,512]{1,0,2:T(8,128)(2,1)} copy(bf16[16,384,512]{1,2,0:T(8,128)(2,1)} %get-tuple-element.987) | data formatting | bytes 12582912 | tf_op jit(solution)/shard_map
  450.9 10.5 %reshape_reshape.3 = bf16[48,128,32,16]{1,0,3,2:T(8,128)(2,1)} reshape(bf16[16,384,512]{1,0,2:T(8,128)(2,1)} %copy.92) | data formatting | bytes 12582912 | tf_op jit(solution)/shard_map/cond/branch_1_fun/reshape;reshape | solution.py:64
  470.9 5.5 fusion.131
  479.5 3.4 fusion.5
  483.0 15.1 %fusion.132 = (bf16[3,128,32,16]{1,0,3,2:T(4,128)(2,1)}, bf16[3,128,32,16]{1,0,3,2:T(4,128)(2,1)S(1)}, bf16[3,128,32,16]{1,0,3,2:T(4,128)(2,1)S(1)}, bf16[3,128,...) fusion(bf16[48,128,32,16]{1,0,3,2:T(8,128)(2,1)} %reshape_reshape.3), kind=kLoop, calls=%fused_computation.210 | loop fusion | bytes 14942208 | tf_op jit(solution)/shard_map/cond/branch_1_fun/slice | solution.py:74
  498.1 3.4 fusion.7
  501.6 3.4 fusion.9
  508.2 3.4 fusion.11
  512.7 3.4 fusion.13
  517.2 3.4 fusion.15
  523.8 3.4 fusion.17
  528.3 3.4 fusion.19
  532.8 3.4 fusion.21
  539.3 3.4 fusion.23
  543.9 3.4 fusion.25
  548.4 3.4 fusion.27
  555.1 3.4 fusion.29
  559.6 3.4 fusion.31
  564.1 3.4 fusion.33
  570.7 3.4 fusion.35
  575.2 3.4 fusion.37
  579.7 3.4 fusion.39
  590.7 3.4 fusion.43
  595.3 3.4 fusion.45
  601.9 3.4 fusion.47
  606.4 3.4 fusion.49
  610.9 3.4 fusion.51
  617.6 3.4 fusion.53
  622.2 3.5 fusion.55
  626.7 3.4 fusion.57
  633.3 3.4 fusion.59
  636.7 9.6 %fusion.133 = (bf16[3,128,32,16]{1,0,3,2:T(4,128)(2,1)}, bf16[3,128,32,16]{1,0,3,2:T(4,128)(2,1)S(1)}, bf16[3,128,32,16]{1,0,3,2:T(4,128)(2,1)S(1)}, bf16[3,128,...) fusion(bf16[48,128,32,16]{1,0,3,2:T(8,128)(2,1)} %reshape_reshape.3), kind=kLoop, calls=%fused_computation.211 | loop fusion | bytes 8650752 | tf_op jit(solution)/shard_map/cond/branch_1_fun/slice | solution.py:74
  646.4 3.4 fusion.61
  649.8 3.4 fusion.63
  656.4 3.4 fusion.65
  660.9 3.4 fusion.67
  665.4 3.4 fusion.69
  672.0 3.4 fusion.71
  676.5 3.4 fusion.73
  681.0 3.4 fusion.75
  687.9 3.4 fusion.77
  692.5 3.4 fusion.79
  697.0 3.4 fusion.81
  703.5 3.4 fusion.83
  708.1 3.4 fusion.85
  712.6 3.4 fusion.87
  719.1 3.4 fusion.89
  723.6 3.4 fusion.91
  728.1 3.4 fusion.93
  737.2 12.7 %bitcast_add_fusion = f32[3,128,32,16]{1,3,2,0:T(8,128)S(1)} fusion(f32[3,128,32,16]{1,3,2,0:T(8,128)S(1)} %fusion.100, f32[32,128,3,16]{1,3,2,0:T(8,128)} %bitcast.516, f32[32,128,3,16]{1,3,2,0:T(8,128)} %bitcast.517, f32[32,128,3,16]{1,3,2,0:T(8,128)} %bitcast.518, f32[32,128,3,16]{1,3,2,0:T(8,128)} %bitcast.519, f32[32,128,3,16]{1,3,2,0:T(8,128)} %bitcast.520, ...), kind=kLoop, calls=%fused_computation.104 | loop fusion | flops 9043968 | bytes 37748736 | tf_op jit(solution)/shard_map/cond/branch_1_fun/add | solution.py:77
  765.8 3.4 collective-permute-done.5
  (131 shorter events, 130.2 us)
Async XLA Ops:
  1.3 14.8 %collective-permute-start.1 = (bf16[2,512]{1,0:T(2,128)(2,1)S(1)}, bf16[2,512]{1,0:T(2,128)(2,1)S(1)}, u32[]{:S(2)}, u32[]{:S(2)}) collective-permute-start(bf16[2,512]{1,0:T(2,128)(2,1)S(1)} %slice.1854), channel_id=1, source_target_pairs={{0,8},{8,16},{16,24},{24,32},{32,40},{40,48},{48,56},{56,64},{64,7... | collective-permute-start | bytes 6152 | tf_op jit(solution)/shard_map/ppermute | solution.py:24
  10.0 11.3 %all-to-all-start = ((bf16[48,8,512]{2,0,1:T(8,128)(2,1)}), bf16[48,8,512]{2,0,1:T(8,128)(2,1)S(1)}, u32[]{:S(2)}, u32[]{:S(2)}) async-start(bf16[48,8,512]{2,0,1:T(8,128)(2,1)} %bitcast.511), calls=%async_computation | async-start | bytes 786432 | tf_op jit(solution)/shard_map/all_to_all | solution.py:88
  16.1 113.3 %copy-start.4 = (f32[1,1,512]{2,1,0:T(1,128)}, f32[1,1,512]{2,1,0:T(1,128)S(1)}, u32[]{:S(2)}) copy-start(f32[1,1,512]{2,1,0:T(1,128)S(1)} %get-tuple-element.1054) | copy-start | bytes 6148
  16.1 113.3 %copy-start.5 = (f32[1,1,512]{2,1,0:T(1,128)}, f32[1,1,512]{2,1,0:T(1,128)S(1)}, u32[]{:S(2)}) copy-start(f32[1,1,512]{2,1,0:T(1,128)S(1)} %get-tuple-element.1055) | copy-start | bytes 6148
  16.1 113.3 %copy-start.6 = (f32[1,1,512]{2,1,0:T(1,128)}, f32[1,1,512]{2,1,0:T(1,128)S(1)}, u32[]{:S(2)}) copy-start(f32[1,1,512]{2,1,0:T(1,128)S(1)} %get-tuple-element.1056) | copy-start | bytes 6148
  22.7 106.7 %copy-start.2 = (f32[384,512]{1,0:T(8,128)}, f32[384,512]{1,0:T(8,128)S(1)}, u32[]{:S(2)}) copy-start(f32[384,512]{1,0:T(8,128)S(1)} %get-tuple-element.1049) | copy-start | bytes 2359300
  26.4 103.0 %all-to-all-start.1 = ((bf16[16,384,512]{1,2,0:T(8,128)(2,1)}), bf16[16,384,512]{1,2,0:T(8,128)(2,1)}, u32[]{:S(2)}, u32[]{:S(2)}) async-start(bf16[16,384,512]{1,2,0:T(8,128)(2,1)} %stack.2), calls=%async_computation.1 | async-start | bytes 12582912 | tf_op jit(solution)/shard_map/all_to_all | solution.py:14
  34.8 25.2 %collective-permute-start.4 = (bf16[2,512]{1,0:T(2,128)(2,1)S(1)}, bf16[2,512]{1,0:T(2,128)(2,1)S(1)}, u32[]{:S(2)}, u32[]{:S(2)}) collective-permute-start(bf16[2,512]{1,0:T(2,128)(2,1)S(1)} %slice.1870), channel_id=1, source_target_pairs={{0,8},{8,16},{16,24},{24,32},{32,40},{40,48},{48,56},{56,64},{64,7... | collective-permute-start | bytes 6152 | tf_op jit(solution)/shard_map/ppermute | solution.py:24
  40.6 21.4 %collective-permute-start.2 = (bf16[2,512]{1,0:T(2,128)(2,1)S(1)}, bf16[2,512]{1,0:T(2,128)(2,1)S(1)}, u32[]{:S(2)}, u32[]{:S(2)}) collective-permute-start(bf16[2,512]{1,0:T(2,128)(2,1)S(1)} %slice.1859), channel_id=1, source_target_pairs={{0,8},{8,16},{16,24},{24,32},{32,40},{40,48},{48,56},{56,64},{64,7... | collective-permute-start | bytes 6152 | tf_op jit(solution)/shard_map/ppermute | solution.py:24
  64.7 696.4 %collective-permute-start = (f32[2,512]{1,0:T(2,128)}, f32[2,512]{1,0:T(2,128)}, u32[]{:S(2)}, u32[]{:S(2)}) collective-permute-start(f32[2,512]{1,0:T(2,128)} %slice.1964), channel_id=1, source_target_pairs={{8,0},{16,8},{24,16},{32,24},{40,32},{48,40},{56,48},{64,56},{72,6... | collective-permute-start | bytes 12296 | tf_op jit(solution)/shard_map/ppermute | solution.py:24
  129.3 627.3 %copy-start = (f32[386,512]{1,0:T(8,128)S(1)}, f32[386,512]{1,0:T(8,128)}, u32[]{:S(2)}) copy-start(f32[386,512]{1,0:T(8,128)} %maximum_convert_fusion.2) | copy-start | bytes 2371588
  129.3 627.3 %copy-start.1 = (f32[386,512]{1,0:T(8,128)S(1)}, f32[386,512]{1,0:T(8,128)}, u32[]{:S(2)}) copy-start(f32[386,512]{1,0:T(8,128)} %maximum_convert_fusion.1) | copy-start | bytes 2371588
  129.3 627.3 %copy-start.7 = (f32[1,1,512]{2,1,0:T(1,128)S(1)}, f32[1,1,512]{2,1,0:T(1,128)}, u32[]{:S(2)}) copy-start(f32[1,1,512]{2,1,0:T(1,128)} %get-tuple-element.1051) | copy-start | bytes 6148
  129.4 627.3 %copy-start.8 = (f32[1,1,512]{2,1,0:T(1,128)S(1)}, f32[1,1,512]{2,1,0:T(1,128)}, u32[]{:S(2)}) copy-start(f32[1,1,512]{2,1,0:T(1,128)} %get-tuple-element.1052) | copy-start | bytes 6148
  129.4 627.3 %copy-start.9 = (f32[1,1,512]{2,1,0:T(1,128)S(1)}, f32[1,1,512]{2,1,0:T(1,128)}, u32[]{:S(2)}) copy-start(f32[1,1,512]{2,1,0:T(1,128)} %get-tuple-element.1053) | copy-start | bytes 6148
  129.4 627.3 %copy-start.10 = (f32[1,1,512]{2,1,0:T(1,128)S(1)}, f32[1,1,512]{2,1,0:T(1,128)}, u32[]{:S(2)}) copy-start(f32[1,1,512]{2,1,0:T(1,128)} %get-tuple-element.1050) | copy-start | bytes 6148
  129.4 627.3 %copy-start.11 = (f32[1,1,512]{2,1,0:T(1,128)S(1)}, f32[1,1,512]{2,1,0:T(1,128)}, u32[]{:S(2)}) copy-start(f32[1,1,512]{2,1,0:T(1,128)} %get-tuple-element.1057) | copy-start | bytes 6148
  129.4 627.3 %copy-start.12 = (f32[1,1,512]{2,1,0:T(1,128)S(1)}, f32[1,1,512]{2,1,0:T(1,128)}, u32[]{:S(2)}) copy-start(f32[1,1,512]{2,1,0:T(1,128)} %get-tuple-element.1058) | copy-start | bytes 6148
  129.4 631.6 %copy-start.3 = (f32[384,512]{1,0:T(8,128)S(1)}, f32[384,512]{1,0:T(8,128)}, u32[]{:S(2)}) copy-start(f32[384,512]{1,0:T(8,128)} %copy-done.2) | copy-start | bytes 2359300
  758.3 6.4 collective-permute-start.3
  762.8 6.4 collective-permute-start.5
